TPU v7x, 512 devices: a whole 4x8x8 slice. The times are simulated.
512 devices in a mesh: pencil: 128 (over y, z, core), lev: 4 (over x).
Axes of the slice: x: 4, y: 8, z: 8, core: 2. Of those that a mesh axis runs over, the one named last changes fastest.
Arguments:
- background_std: float32 [4, 4096, 2048], P('lev', 'pencil'), may hold values from 0.4 to 6.1
- x_kernel: float32 [4, 31], P('lev'), may hold values from -0.06 to 0.12
- y_kernel: float32 [4, 31], P('lev'), may hold values from -0.06 to 0.12
- obs_owner: int32 [131072, 1], P(('pencil', 'lev')), may hold values from 0 to 127; in each aligned block of 256 rows (0 to 255, 256 to 511, ...) at most 4 rows name the same one
- obs_cells: int32 [131072, 16], P(('pencil', 'lev')), may hold values from 0 to 65535, as said below
- obs_weights: float32 [131072, 16], P(('pencil', 'lev')), may hold values from -0.05 to 0.2
- innovation: float32 [131072], P(('pencil', 'lev')), may hold values from -6 to 6
- obs_precision: float32 [131072], P(('pencil', 'lev')), may hold values from 0.25 to 4
- obs_counts: int32 [512], P(('pencil', 'lev')), may hold values from 129 to 256, as said below
Outputs:
- control: float32 [4, 2048, 4096], P('lev', 'pencil')
- increment: float32 [4, 4096, 2048], P('lev', 'pencil')
Inputs may be any that keep to these rules, and one draw needn't show every extreme that they name: `obs_owner`: no device holds more than 4 observations of one owner, and some device reaches 4. `obs_cells`: indices into the owner's tile of 1 slabs by 32 columns by 2048 rows, flattened in that order. `obs_counts`: some device has all 256 slots live.
All inputs are finite; a program needn't handle non-finite values.
Results may differ from a plain program's by a relative error of at most 0.0001.
Values sent between devices are 32-bit elements; how exact they have to be, the bound alone decides.
A program may use at most 64 MiB of HBM per device.

v0:
```python
import jax
import jax.numpy as jnp
from jax import lax
from jax.sharding import PartitionSpec as P

ITERS = 2


def smooth(grid_field, kernel_taps, periodic):
    taps = kernel_taps.shape[1]
    margin = taps // 2
    length = grid_field.shape[2]
    if periodic:
        padded = jnp.concatenate(
            [grid_field[:, :, length - margin :], grid_field, grid_field[:, :, :margin]], axis=2
        )
    else:
        padded = jnp.pad(grid_field, ((0, 0), (0, 0), (margin, margin)))
    result = jnp.zeros(grid_field.shape, jnp.float32)
    for offset in range(taps):
        result = (
            result + kernel_taps[:, offset][:, None, None] * padded[:, :, offset : offset + length]
        )
    return result


def total_squares(values):
    return lax.psum(jnp.sum(values * values), ("pencil", "lev"))


def body(
    background_std,
    x_kernel,
    y_kernel,
    obs_owner,
    obs_cells,
    obs_weights,
    innovation,
    obs_precision,
    obs_counts,
):
    pencils = lax.axis_size("pencil")
    slab_count, columns, height = background_std.shape
    holding = obs_owner.shape[0]
    stencil_size = obs_cells.shape[1]
    capacity = 2 * holding // pencils
    ordinal = jnp.arange(holding, dtype=jnp.int32)
    living = (ordinal < obs_counts[0]).astype(jnp.float32)
    target = obs_owner[:, 0]
    member = (target[:, None] == jnp.arange(pencils, dtype=jnp.int32)[None, :]).astype(jnp.int32)
    earlier = jnp.cumsum(member, axis=0) - member
    slot_index = target * capacity + jnp.sum(earlier * member, axis=1)
    packed = jnp.concatenate(
        [obs_weights, innovation[:, None], (obs_precision * living)[:, None]], axis=1
    )
    send_values = (
        jnp.zeros((pencils * capacity, packed.shape[1]), jnp.float32).at[slot_index].set(packed)
    )
    send_cells = (
        jnp.zeros((pencils * capacity, stencil_size), jnp.int32).at[slot_index].set(obs_cells)
    )
    recv_cells, recv_values = (
        lax.all_to_all(
            send_cells.reshape(pencils, capacity, stencil_size),
            "pencil",
            split_axis=0,
            concat_axis=0,
            tiled=True,
        ),
        lax.all_to_all(
            send_values.reshape(pencils, capacity, packed.shape[1]),
            "pencil",
            split_axis=0,
            concat_axis=0,
            tiled=True,
        ),
    )
    stencil = recv_cells.reshape(-1, stencil_size)
    received = recv_values.reshape(-1, packed.shape[1])
    interp = received[:, :stencil_size]
    departure = received[:, stencil_size]
    weight = received[:, stencil_size + 1]

    def spread(values):
        total = jnp.zeros((slab_count * columns * height,), jnp.float32)
        total = total.at[stencil.reshape(-1)].add((interp * values[:, None]).reshape(-1))
        return total.reshape(slab_count, columns, height)

    def forward(grid_field):
        along_x = smooth(grid_field, x_kernel, True)
        turned = lax.all_to_all(along_x, "pencil", split_axis=2, concat_axis=1, tiled=True)
        return background_std * smooth(jnp.swapaxes(turned, 1, 2), y_kernel, False)

    def adjoint(column_field):
        along_y = smooth(background_std * column_field, y_kernel[:, ::-1], False)
        turned = lax.all_to_all(
            jnp.swapaxes(along_y, 1, 2), "pencil", split_axis=1, concat_axis=2, tiled=True
        )
        return smooth(turned, x_kernel[:, ::-1], True)

    gradient_rhs = adjoint(spread(weight * departure))
    control = jnp.zeros_like(gradient_rhs)
    resid = gradient_rhs
    direction = gradient_rhs
    norm_now = total_squares(resid)
    for iteration in range(ITERS):
        smoothed = forward(direction)
        image = direction + adjoint(
            spread(weight * jnp.sum(interp * smoothed.reshape(-1)[stencil], axis=1))
        )
        step_length = norm_now / lax.psum(jnp.sum(direction * image), ("pencil", "lev"))
        control = control + step_length * direction
        resid = resid - step_length * image
        norm_next = total_squares(resid)
        direction = resid + norm_next / norm_now * direction
        norm_now = norm_next
    increment = forward(control)
    return (control, increment)


def solution(mesh):
    return jax.shard_map(
        body,
        mesh=mesh,
        in_specs=(
            P("lev", "pencil", None),
            P("lev", None),
            P("lev", None),
            P(("pencil", "lev"), None),
            P(("pencil", "lev"), None),
            P(("pencil", "lev"), None),
            P(("pencil", "lev")),
            P(("pencil", "lev")),
            P(("pencil", "lev")),
        ),
        out_specs=(P("lev", "pencil", None), P("lev", "pencil", None)),
        check_vma=False,
    )
```

profile of v0, /device:TPU:1, one launch (start us, length us, event | category | flops | bytes accessed | tf_op | source)
XLA Modules:
  0.0 1134.4 jit_solution(5967069336464141421)
XLA Ops:
  4.1 1.8 scatter_custom_fusion
  5.9 18.4 %all-to-all-start = ((s32[128,4,16]{2,1,0:T(4,128)}), s32[128,4,16]{2,1,0:T(4,128)S(1)}, u32[]{:S(2)}, u32[]{:S(2)}) async-start(s32[128,4,16]{2,1,0:T(4,128)} %bitcast.9), calls=%async_computation | async-start | bytes 524288 | tf_op jit(solution)/shard_map/all_to_all | solution.py:63
  25.0 2.1 fusion.717
  28.6 1.8 scatter_custom_fusion.1
  31.1 7.4 all-to-all-done
  38.6 6.9 all-to-all-start.1
  45.8 14.1 %all-to-all-done.1 = f32[128,4,18]{2,1,0:T(4,128)S(1)} async-done(((f32[128,4,18]{2,1,0:T(4,128)}), f32[128,4,18]{2,1,0:T(4,128)S(1)}, u32[]{:S(2)}, u32[]{:S(2)}) %all-to-all-start.1) | async-done | bytes 36896 | tf_op jit(solution)/shard_map/all_to_all | solution.py:70
  60.4 48.7 %scatter_custom_fusion.2 = f32[65536]{0:T(1024)S(1)} fusion(s32[8192]{0:T(1024)S(1)} %bitcast.179, f32[8192]{0:T(1024)S(1)} %reshape.572, f32[]{:T(128)} %constant.5.clone.1), kind=kCustom, calls=%fused_computation.1140 | custom fusion | flops 8192 | bytes 262148 | tf_op jit(solution)/shard_map/scatter-add | solution.py:86
  109.2 21.3 %add_bitcast_fusion.2 = f32[1,2048,32]{1,2,0:T(8,128)S(1)} fusion(f32[1,32,2048]{2,1,0:T(8,128)S(1)} %mul.1102, f32[]{:T(128)} %bitcast.45, f32[]{:T(128)} %bitcast.44, f32[]{:T(128)} %bitcast.43, f32[]{:T(128)} %bitcast.42, f32[]{:T(128)} %bitcast.41, f32[]{:T(128)} %bitcast.40, f32[]{:T(128)} %bitcast.39, f32[]{:T(128)} %bitcast.38, f32[]{:T(128)} %bitcast.37, ...), kind=kLoop, calls=%fused_computation.1079 | loop fusion | flops 3997696 | bytes 524412 | tf_op jit(solution)/shard_map/transpose | solution.py:97
  131.7 9.4 reduce.6
  141.1 1.2 reshape.607
  142.3 10.2 all-to-all-start.2
  153.9 12.7 %all-to-all-done.2 = f32[128,1,512]{2,1,0:T(1,128)S(1)} async-done(((f32[128,1,512]{2,1,0:T(1,128)}), f32[128,1,512]{2,1,0:T(1,128)S(1)}, u32[]{:S(2)}, u32[]{:S(2)}) %all-to-all-start.2) | async-done | bytes 262176 | tf_op jit(solution)/shard_map/all_to_all | solution.py:96
  166.6 1.3 reduce.7
  167.9 1.8 reshape.608
  170.6 21.4 %fusion.435 = f32[1,16,4096]{2,1,0:T(8,128)S(1)} fusion(f32[1,16,15]{2,1,0:T(8,128)S(1)} %get-tuple-element.20, f32[1,16,15]{2,1,0:T(8,128)S(1)} %get-tuple-element.19, f32[1,16,4096]{2,1,0:T(8,128)S(1)} %all_to_all.89, f32[]{:T(128)} %bitcast.78, f32[]{:T(128)} %bitcast.77, f32[]{:T(128)} %bitcast.76, f32[]{:T(128)} %bitcast.75, f32[]{:T(128)} %bitcast.74, ...), kind=kLoop, calls=%fused_computation.612 | loop fusion | flops 5963776 | bytes 526332 | tf_op jit(solution)/shard_map/add | solution.py:22
  192.1 21.4 %fusion.349 = f32[1,16,4096]{2,1,0:T(8,128)S(1)} fusion(f32[1,16,15]{2,1,0:T(8,128)S(1)} %get-tuple-element.18, f32[1,16,15]{2,1,0:T(8,128)S(1)} %get-tuple-element.17, f32[1,16,4096]{2,1,0:T(8,128)S(1)} %fusion.435, f32[]{:T(128)} %bitcast.78, f32[]{:T(128)} %bitcast.77, f32[]{:T(128)} %bitcast.76, f32[]{:T(128)} %bitcast.75, f32[]{:T(128)} %bitcast.74, ...), kind=kLoop, calls=%fused_computation.526 | loop fusion | flops 5963776 | bytes 526332 | tf_op jit(solution)/shard_map/add | solution.py:22
  213.6 2.5 copy.61
  216.1 19.4 %reduce.8 = f32[4096,16]{1,0:T(8,128)} reduce(f32[4096,1,16]{2,1,0:T(1,128)S(1)} %bitcast.158, f32[]{:T(128)} %broadcast.269), dimensions={1}, to_apply=%bitcast.129.reduce_sub_computation | reduce | bytes 524292
  235.5 3.2 reshape.609
  238.6 6.9 all-to-all-start.3
  245.7 14.1 %all-to-all-done.3 = f32[128,1,512]{2,1,0:T(1,128)S(1)} async-done(((f32[128,1,512]{2,1,0:T(1,128)}), f32[128,1,512]{2,1,0:T(1,128)S(1)}, u32[]{:S(2)}, u32[]{:S(2)}) %all-to-all-start.3) | async-done | bytes 262176 | tf_op jit(solution)/shard_map/all_to_all | solution.py:91
  259.9 1.3 reduce.9
  261.2 3.9 reshape.610
  265.1 1.8 copy.79
  266.9 1.8 copy.63
  269.0 21.3 %multiply_bitcast_fusion.1 = f32[4,16,8,128]{3,2,1,0:T(8,128)S(1)} fusion(f32[1,32,2048]{2,1,0:T(8,128)S(1)} %copy-done, f32[1,32,2048]{2,1,0:T(8,128)S(1)} %bitcast.175, f32[]{:T(128)} %bitcast.45, f32[]{:T(128)} %bitcast.44, f32[]{:T(128)} %bitcast.43, f32[]{:T(128)} %bitcast.42, f32[]{:T(128)} %bitcast.41, f32[]{:T(128)} %bitcast.40, f32[]{:T(128)} %bitcast.39, ...), kind=kLoop, calls=%fused_computation.1036 | loop fusion | flops 4063232 | bytes 786556
  290.4 45.5 %gather_fusion = f32[8192]{0:T(1024)S(1)} fusion(f32[65536]{0:T(1024)S(1)} %bitcast.146, s32[8192]{0:T(1024)S(1)} %broadcast_clamp_fusion), kind=kCustom, calls=%fused_computation | custom fusion | bytes 98304 | tf_op jit(solution)/shard_map/gather | solution.py:109
  336.9 48.6 %scatter_custom_fusion.3 = f32[65536]{0:T(1024)S(1)} fusion(s32[8192]{0:T(1024)S(1)} %bitcast.180, f32[8192]{0:T(1024)S(1)} %reshape.580, f32[]{:T(128)} %constant.5.clone.1), kind=kCustom, calls=%fused_computation.1138 | custom fusion | flops 8192 | bytes 262148 | tf_op jit(solution)/shard_map/scatter-add | solution.py:86
  385.6 21.3 %add_bitcast_fusion.1 = f32[1,2048,32]{1,2,0:T(8,128)S(1)} fusion(f32[1,32,2048]{2,1,0:T(8,128)S(1)} %mul.1354, f32[]{:T(128)} %bitcast.45, f32[]{:T(128)} %bitcast.44, f32[]{:T(128)} %bitcast.43, f32[]{:T(128)} %bitcast.42, f32[]{:T(128)} %bitcast.41, f32[]{:T(128)} %bitcast.40, f32[]{:T(128)} %bitcast.39, f32[]{:T(128)} %bitcast.38, f32[]{:T(128)} %bitcast.37, ...), kind=kLoop, calls=%fused_computation.992 | loop fusion | flops 3997696 | bytes 524412 | tf_op jit(solution)/shard_map/transpose | solution.py:97
  407.5 9.4 reduce.10
  417.3 23.6 %all_to_all.118 = f32[128,1,512]{2,1,0:T(1,128)S(1)} all-to-all(f32[128,1,512]{2,1,0:T(1,128)S(1)} %reshape.611), channel_id=1, replica_groups=mesh['pencil'=128,'lev'=4] {'pencil'}, dimensions={0} | all-to-all | bytes 524288 | tf_op jit(solution)/shard_map/all_to_all | solution.py:96
  441.0 1.3 reduce.11
  442.3 1.8 reshape.612
  445.0 22.1 %multiply_reduce_fusion.3 = (f32[]{:T(128)}, f32[]{:T(128)}, f32[1,16,4096]{2,1,0:T(8,128)S(1)}) fusion(f32[1,16,4096]{2,1,0:T(8,128)S(1)} %fusion.435, f32[1,16,15]{2,1,0:T(8,128)S(1)} %get-tuple-element.16, f32[1,16,4096]{2,1,0:T(8,128)S(1)} %all_to_all.97, f32[]{:T(128)} %bitcast.78, f32[]{:T(128)} %bitcast.77, f32[]{:T(128)} %bitcast.76, f32[]{:T(128)} %bitcast.75, ...), kind=kLoop, calls=%fused_computation.991 | loop fusion | flops 6291454 | bytes 788484 | tf_op jit(solution)/shard_map/reduce_sum | solution.py:111
  467.1 96.1 %all-reduce.6 = (f32[]{:T(128)}, f32[]{:T(128)}) all-reduce(f32[]{:T(128)} %get-tuple-element.5, f32[]{:T(128)} %get-tuple-element.4), channel_id=1, replica_groups=mesh['pencil'=128,'lev'=4] {'pencil','lev'}, use_global_device_ids=true, to_apply=%region_7.8 | all-reduce | flops 2 | bytes 16 | tf_op jit(solution)/shard_map/psum | solution.py:28
  565.1 94.7 %psum.30 = f32[]{:T(128)} all-reduce(f32[]{:T(128)} %multiply_reduce_fusion.2), channel_id=1, replica_groups=mesh['pencil'=128,'lev'=4] {'pencil','lev'}, use_global_device_ids=true, to_apply=%region_13.14 | all-reduce | flops 1 | bytes 8 | tf_op jit(solution)/shard_map/psum | solution.py:28
  661.3 21.4 %fusion.176 = f32[1,16,4096]{2,1,0:T(8,128)S(1)} fusion(f32[1,16,15]{2,1,0:T(8,128)S(1)} %get-tuple-element.14, f32[1,16,15]{2,1,0:T(8,128)S(1)} %get-tuple-element.13, f32[1,16,4096]{2,1,0:T(8,128)S(1)} %multiply_add_fusion.1, f32[]{:T(128)} %bitcast.78, f32[]{:T(128)} %bitcast.77, f32[]{:T(128)} %bitcast.76, f32[]{:T(128)} %bitcast.75, f32[]{:T(128)} %bitcast.74, ...), kind=kLoop, calls=%fused_computation.353 | loop fusion | flops 5963776 | bytes 526332 | tf_op jit(solution)/shard_map/add | solution.py:22
  682.8 2.5 copy.68
  685.2 19.4 %reduce.12 = f32[4096,16]{1,0:T(8,128)} reduce(f32[4096,1,16]{2,1,0:T(1,128)S(1)} %bitcast.159, f32[]{:T(128)} %broadcast.269), dimensions={1}, to_apply=%bitcast.133.reduce_sub_computation | reduce | bytes 524292
  704.7 2.4 reshape.613
  707.1 24.2 %all_to_all.119 = f32[128,1,512]{2,1,0:T(1,128)S(1)} all-to-all(f32[128,1,512]{2,1,0:T(1,128)S(1)} %reshape.613), channel_id=1, replica_groups=mesh['pencil'=128,'lev'=4] {'pencil'}, dimensions={0} | all-to-all | bytes 524288 | tf_op jit(solution)/shard_map/all_to_all | solution.py:91
  731.3 1.3 reduce.13
  732.6 3.9 reshape.614
  736.5 1.8 copy.80
  738.3 1.8 copy.70
  740.4 21.3 %multiply_bitcast_fusion = f32[4,16,8,128]{3,2,1,0:T(8,128)S(1)} fusion(f32[1,32,2048]{2,1,0:T(8,128)S(1)} %copy-done, f32[1,32,2048]{2,1,0:T(8,128)S(1)} %bitcast.176, f32[]{:T(128)} %bitcast.45, f32[]{:T(128)} %bitcast.44, f32[]{:T(128)} %bitcast.43, f32[]{:T(128)} %bitcast.42, f32[]{:T(128)} %bitcast.41, f32[]{:T(128)} %bitcast.40, f32[]{:T(128)} %bitcast.39, ...), kind=kLoop, calls=%fused_computation.946 | loop fusion | flops 4063232 | bytes 786556
  761.8 45.5 %gather_fusion.1 = f32[8192]{0:T(1024)S(1)} fusion(f32[65536]{0:T(1024)S(1)} %bitcast.145, s32[8192]{0:T(1024)S(1)} %broadcast_clamp_fusion), kind=kCustom, calls=%fused_computation.1 | custom fusion | bytes 98304 | tf_op jit(solution)/shard_map/gather | solution.py:109
  808.3 48.6 %scatter_custom_fusion.4 = f32[65536]{0:T(1024)S(1)} fusion(s32[8192]{0:T(1024)S(1)} %bitcast.181, f32[8192]{0:T(1024)S(1)} %reshape.588, f32[]{:T(128)} %constant.5.clone.1), kind=kCustom, calls=%fused_computation.1136 | custom fusion | flops 8192 | bytes 262148 | tf_op jit(solution)/shard_map/scatter-add | solution.py:86
  857.0 21.3 %add_bitcast_fusion = f32[1,2048,32]{1,2,0:T(8,128)S(1)} fusion(f32[1,32,2048]{2,1,0:T(8,128)S(1)} %mul.1492, f32[]{:T(128)} %bitcast.45, f32[]{:T(128)} %bitcast.44, f32[]{:T(128)} %bitcast.43, f32[]{:T(128)} %bitcast.42, f32[]{:T(128)} %bitcast.41, f32[]{:T(128)} %bitcast.40, f32[]{:T(128)} %bitcast.39, f32[]{:T(128)} %bitcast.38, f32[]{:T(128)} %bitcast.37, ...), kind=kLoop, calls=%fused_computation.902 | loop fusion | flops 3997696 | bytes 524412 | tf_op jit(solution)/shard_map/transpose | solution.py:97
  878.9 9.4 reduce.14
  888.7 23.2 %all_to_all.120 = f32[128,1,512]{2,1,0:T(1,128)S(1)} all-to-all(f32[128,1,512]{2,1,0:T(1,128)S(1)} %reshape.615), channel_id=1, replica_groups=mesh['pencil'=128,'lev'=4] {'pencil'}, dimensions={0} | all-to-all | bytes 524288 | tf_op jit(solution)/shard_map/all_to_all | solution.py:96
  911.9 1.3 reduce.15
  913.3 1.8 reshape.616
  916.0 22.0 %fusion = f32[]{:T(128)} fusion(f32[1,16,4096]{2,1,0:T(8,128)S(1)} %multiply_add_fusion.1, f32[1,16,15]{2,1,0:T(8,128)S(1)} %get-tuple-element.12, f32[1,16,15]{2,1,0:T(8,128)S(1)} %get-tuple-element.11, f32[1,16,4096]{2,1,0:T(8,128)S(1)} %all_to_all.105, f32[]{:T(128)} %bitcast.78, f32[]{:T(128)} %bitcast.77, f32[]{:T(128)} %bitcast.76, f32[]{:T(128)} %bitcast.75, ...), kind=kLoop, calls=%fused_computation.177 | loop fusion | flops 6160383 | bytes 526336 | tf_op jit(solution)/shard_map/reduce_sum | solution.py:111
  938.0 95.7 %psum.31 = f32[]{:T(128)} all-reduce(f32[]{:T(128)} %fusion), channel_id=1, replica_groups=mesh['pencil'=128,'lev'=4] {'pencil','lev'}, use_global_device_ids=true, to_apply=%region_17.18 | all-reduce | flops 1 | bytes 8 | tf_op jit(solution)/shard_map/psum | solution.py:111
  1035.8 21.4 %fusion.4 = f32[1,16,4096]{2,1,0:T(8,128)S(1)} fusion(f32[1,16,15]{2,1,0:T(8,128)S(1)} %get-tuple-element.10, f32[1,16,15]{2,1,0:T(8,128)S(1)} %get-tuple-element.9, f32[1,16,4096]{2,1,0:T(8,128)S(1)} %multiply_add_fusion, f32[]{:T(128)} %bitcast.78, f32[]{:T(128)} %bitcast.77, f32[]{:T(128)} %bitcast.76, f32[]{:T(128)} %bitcast.75, f32[]{:T(128)} %bitcast.74, ...), kind=kLoop, calls=%fused_computation.181 | loop fusion | flops 5963776 | bytes 526332 | tf_op jit(solution)/shard_map/add | solution.py:22
  1057.3 2.5 copy.75
  1059.7 19.4 %reduce.16 = f32[4096,16]{1,0:T(8,128)} reduce(f32[4096,1,16]{2,1,0:T(1,128)S(1)} %bitcast.160, f32[]{:T(128)} %broadcast.269), dimensions={1}, to_apply=%bitcast.137.reduce_sub_computation | reduce | bytes 524292
  1079.2 2.4 reshape.617
  1081.6 23.5 %all_to_all.121 = f32[128,1,512]{2,1,0:T(1,128)S(1)} all-to-all(f32[128,1,512]{2,1,0:T(1,128)S(1)} %reshape.617), channel_id=1, replica_groups=mesh['pencil'=128,'lev'=4] {'pencil'}, dimensions={0} | all-to-all | bytes 524288 | tf_op jit(solution)/shard_map/all_to_all | solution.py:91
  1105.1 1.3 reduce.17
  1106.4 3.9 reshape.618
  1112.2 22.0 %add_multiply_fusion.1 = f32[1,32,2048]{2,1,0:T(8,128)} fusion(f32[1,32,2048]{2,1,0:T(8,128)S(1)} %copy-done, f32[1,32,2048]{2,1,0:T(8,128)S(1)} %bitcast.174, f32[]{:T(128)} %bitcast.45, f32[]{:T(128)} %bitcast.44, f32[]{:T(128)} %bitcast.43, f32[]{:T(128)} %bitcast.42, f32[]{:T(128)} %bitcast.41, f32[]{:T(128)} %bitcast.40, f32[]{:T(128)} %bitcast.39, ...), kind=kLoop, calls=%fused_computation.859 | loop fusion | flops 4063232 | bytes 786556 | tf_op jit(solution)/shard_map/mul | solution.py:92
  (79 shorter events, 20.3 us)
Async XLA Ops:
  0.6 29.8 %copy-start.2 = (f32[1,31]{1,0:T(1,128)S(1)}, f32[1,31]{1,0:T(1,128)}, u32[]{:S(2)}) copy-start(f32[1,31]{1,0:T(1,128)} %param.11) | copy-start | bytes 376
  4.1 105.1 %copy-start = (f32[1,32,2048]{2,1,0:T(8,128)S(1)}, f32[1,32,2048]{2,1,0:T(8,128)}, u32[]{:S(2)}) copy-start(f32[1,32,2048]{2,1,0:T(8,128)} %param.9) | copy-start | bytes 786436
  5.9 32.6 %all-to-all-start = ((s32[128,4,16]{2,1,0:T(4,128)}), s32[128,4,16]{2,1,0:T(4,128)S(1)}, u32[]{:S(2)}, u32[]{:S(2)}) async-start(s32[128,4,16]{2,1,0:T(4,128)} %bitcast.9), calls=%async_computation | async-start | bytes 524288 | tf_op jit(solution)/shard_map/all_to_all | solution.py:63
  38.6 21.3 %all-to-all-start.1 = ((f32[128,4,18]{2,1,0:T(4,128)}), f32[128,4,18]{2,1,0:T(4,128)S(1)}, u32[]{:S(2)}, u32[]{:S(2)}) async-start(f32[128,4,18]{2,1,0:T(4,128)} %bitcast.14), calls=%async_computation.1 | async-start | bytes 524288 | tf_op jit(solution)/shard_map/all_to_all | solution.py:70
  131.1 21.3 %copy-start.3 = (f32[1,31]{1,0:T(1,128)S(1)}, f32[1,31]{1,0:T(1,128)}, u32[]{:S(2)}) copy-start(f32[1,31]{1,0:T(1,128)} %param.10) | copy-start | bytes 376
  142.3 24.3 %all-to-all-start.2 = ((f32[128,1,512]{2,1,0:T(1,128)}), f32[128,1,512]{2,1,0:T(1,128)S(1)}, u32[]{:S(2)}, u32[]{:S(2)}) async-start(f32[128,1,512]{2,1,0:T(1,128)} %reshape.607), calls=%async_computation.2 | async-start | bytes 524288 | tf_op jit(solution)/shard_map/all_to_all | solution.py:96
  238.6 21.2 %all-to-all-start.3 = ((f32[128,1,512]{2,1,0:T(1,128)}), f32[128,1,512]{2,1,0:T(1,128)S(1)}, u32[]{:S(2)}, u32[]{:S(2)}) async-start(f32[128,1,512]{2,1,0:T(1,128)} %reshape.609), calls=%async_computation.3 | async-start | bytes 524288 | tf_op jit(solution)/shard_map/all_to_all | solution.py:91
  1035.1 0.7 copy-start.1
where the time goes:
time: 1140 us; the launch traced here: 1130 us
  other arithmetic  504 us (44%)
  blocking collectives  381 us (33%)
  local copies, waits for them, and re-layouts  152 us (13%)
  waiting for transfers between devices  48.3 us (4%)
  starting transfers between devices  42.4 us (4%)
    psum x2, blocking collectives, total_squares(): return lax.psum(jnp.sum(values * values), ('pencil', 'lev'))  191 us
    scatter-add x3, other arithmetic, spread(): total.at[stencil.reshape(-1)].add((interp * values[:, None]).reshape(-1))  146 us
    unnamed x8, other arithmetic  129 us
    psum x1, blocking collectives, body(): lax.psum(jnp.sum(direction * image), ('pencil', 'lev'))  95.7 us
    gather x4, local copies, waits for them, and re-layouts, body(): smoothed.reshape(-1)[stencil]  91.3 us
    add x4, other arithmetic, smooth(): result + kernel_taps[:, offset][:, None, None] * padded[:, :, offset:offs...  85.8 us
    transpose x3, other arithmetic, adjoint(): jnp.swapaxes(along_y, 1, 2)  63.9 us
    all_to_all x2, blocking collectives, forward(): lax.all_to_all(along_x, 'pencil', split_axis=2, concat_axis=1, tiled=True)  47.7 us
  transfers between devices with their start and end apart: 4, of which 4 were waited for; matrix products, arithmetic and copies ran while one was open for 1% of the time, Pallas kernels for 0%

commit v1 on v0

v1 whole, which is shorter than its diff:
```python
import functools

import jax
import jax.numpy as jnp
from jax import lax
from jax.experimental import pallas as pl
from jax.experimental.pallas import tpu as pltpu
from jax.sharding import PartitionSpec as P

F32, BF16, I32 = jnp.float32, jnp.bfloat16, jnp.int32
MESH = pl.DeviceIdType.MESH
HALF = 15
PENCILS = 128
LEVS = 4
NEAR = 16
FAR_Y = 8
SLOTS = 4
NT = (((1,), (1,)), ((), ()))


def dot(a, b):
    return jnp.dot(a, b, preferred_element_type=F32)


def pieces(v):
    hi = v.astype(BF16)
    return hi, (v - hi.astype(F32)).astype(BF16)


def band(delta, taps, sign):
    out = jnp.zeros(delta.shape, F32)
    for d in range(-HALF, HALF + 1):
        out = jnp.where(delta == d, taps[0, HALF + sign * d], out)
    return out


def lane_blocks(x):
    lane = lax.broadcasted_iota(I32, x[0].shape, x[0].ndim - 1)
    ax = x[0].ndim - 1
    low, even = lane < 64, (lane & 32) == 0

    def halves(a, b):
        return jnp.where(low, a, pltpu.roll(b, 64, ax)), jnp.where(low, pltpu.roll(a, 64, ax), b)

    def quarters(a, b):
        return jnp.where(even, a, pltpu.roll(b, 32, ax)), jnp.where(even, pltpu.roll(a, 96, ax), b)

    a, c = halves(x[0], x[2])
    b, d = halves(x[1], x[3])
    return quarters(a, b) + quarters(c, d)


def kernel(
    std_in, xk, yk, owner, cells, weights, innov, prec, counts,
    control_out, incr_out,
    osend, orecv, rt_ref, hi_ref, lo_ref, w_ref, lot,
    ty, tyt, ax_ref, std, g2, acc,
    fown, fl, fr, vbuf, bbuf, ubuf, bb_f, bu_f,
    xsend, xrecv, asend, arecv, csend, crecv,
    osem, hsem_s, hsem_r, xsem, asem, csem, lsem,
):
    me = lax.axis_index("pencil")
    lev = lax.axis_index("lev")
    near = lax.rem(me, NEAR)
    row = lax.div(me, NEAR)
    left, right = lax.rem(me + PENCILS - 1, PENCILS), lax.rem(me + 1, PENCILS)

    barrier = pltpu.get_barrier_semaphore()

    @pl.loop(1, PENCILS)
    def _(i):
        pl.semaphore_signal(barrier, inc=1, device_id=(lax.rem(me + i, PENCILS), lev), device_id_type=MESH)

    @pl.loop(FAR_Y, FAR_Y * LEVS)
    def _(i):
        pl.semaphore_signal(
            barrier,
            inc=1,
            device_id=(lax.rem(row + i, FAR_Y) * NEAR + near, lax.rem(lev + lax.div(i, FAR_Y), LEVS)),
            device_id_type=MESH,
        )

    n_obs = cells.shape[1]
    lane_o = lax.broadcasted_iota(I32, (1, n_obs), 1)
    weight = jnp.where(lane_o < counts[0], prec[...], 0.0)
    member = lax.broadcasted_iota(I32, (PENCILS, n_obs), 0) == owner[...]
    member_b = jnp.where(member, 1.0, 0.0).astype(BF16)
    before = lax.broadcasted_iota(I32, (n_obs, n_obs), 0) < lax.broadcasted_iota(I32, (n_obs, n_obs), 1)
    rank = dot(member_b, jnp.where(before, 1.0, 0.0).astype(BF16))
    sub8 = lax.broadcasted_iota(I32, (8, n_obs), 0)
    tail = jnp.where(sub8 == 0, weight * innov[...], jnp.where(sub8 == 1, weight, 0.0))
    feats = jnp.concatenate(
        [cells[...].astype(F32), weights[...], tail, jnp.zeros((24, n_obs), F32)], axis=0
    )
    f0 = feats.astype(BF16)
    rest = feats - f0.astype(F32)
    f1 = rest.astype(BF16)
    f2 = (rest - f1.astype(F32)).astype(BF16)
    packed = []
    for s in range(SLOTS):
        pick = jnp.where(member, jnp.where(rank == float(s), 1.0, 0.0), 0.0).astype(BF16)
        parts = [lax.dot_general(pick, f, NT, preferred_element_type=F32) for f in (f0, f1, f2)]
        packed.append(parts[0] + parts[1] + parts[2])
    for h in range(2):
        osend[pl.ds(h, PENCILS, stride=2), :] = jnp.concatenate(packed[2 * h : 2 * h + 2], axis=1)

    pl.semaphore_wait(barrier, PENCILS - 1 + FAR_Y * (LEVS - 1))

    own = pltpu.make_async_copy(osend.at[pl.ds(me * 2, 2)], orecv.at[pl.ds(me * 2, 2)], lsem.at[0])
    own.start()

    def obs_copy(q, n=1):
        return pltpu.make_async_remote_copy(
            src_ref=osend.at[pl.ds(q * 2, 2 * n)],
            dst_ref=orecv.at[pl.ds((me if n == 1 else 0) * 2, 2 * n)],
            send_sem=osem.at[0],
            recv_sem=osem.at[1],
            device_id=(q if n == 1 else right, lev),
            device_id_type=MESH,
        )

    @pl.loop(1, PENCILS)
    def _(i):
        obs_copy(lax.rem(me + i, PENCILS)).start()

    base_delta = lax.broadcasted_iota(I32, (8, 512), 0) - lax.broadcasted_iota(I32, (8, 512), 1) + 256
    for sign, ref in ((1, ty), (-1, tyt)):
        base = band(base_delta, yk, sign)
        for g in range(48):
            p0 = 8 * g if g < 40 else 8 * g - 384
            r = pltpu.roll(base, (p0 - 256) % 512, 1)[:, :256]
            acc[8 * g : 8 * g + 8, :] = r
        hi, lo = pieces(acc[0:384, :])
        ref[0:384, :] = hi
        ref[384:768, :] = lo
    delta = lax.broadcasted_iota(I32, (32, 96), 1) - lax.broadcasted_iota(I32, (32, 96), 0) - 32
    delta_w = lax.broadcasted_iota(I32, (96, 96), 1) - lax.broadcasted_iota(I32, (96, 96), 0)
    a1 = band(delta, xk, -1)
    a2 = jnp.dot(
        band(delta, xk, 1),
        band(delta_w, xk, -1),
        preferred_element_type=F32,
        precision=lax.Precision.HIGHEST,
    )
    a_hi, a_lo = pieces(jnp.concatenate([a1, a2], axis=0))
    ax_ref[0:64, :] = a_hi
    ax_ref[64:128, :] = a_lo
    for t in range(8):
        std[t * 32 : t * 32 + 32, :] = std_in[0, :, t * 256 : t * 256 + 256]

    own.wait()
    everyone = obs_copy(0, PENCILS - 1)
    everyone.wait_send()
    everyone.wait_recv()

    for h in range(2):
        rt_ref[h * 128 : h * 128 + 128, :] = orecv[pl.ds(h, PENCILS, stride=2), :].T
    wd, wgt = [], []
    for s in range(SLOTS):
        c = rt_ref[s * 64 : s * 64 + 16, :].astype(I32)
        cols = slice(s * 128, s * 128 + 128)
        hi_ref[:, cols] = (((c >> 8) & 7) * 32 + (c >> 11)).astype(F32)
        lo_ref[:, cols] = (c & 255).astype(F32)
        w_ref[:, cols] = rt_ref[s * 64 + 16 : s * 64 + 32, :]
        wd.append(rt_ref[s * 64 + 32 : s * 64 + 33, :])
        wgt.append(rt_ref[s * 64 + 33 : s * 64 + 34, :])
    wd, wgt = jnp.concatenate(wd, axis=1), jnp.concatenate(wgt, axis=1)
    iota_f = lax.broadcasted_iota(I32, (256, 128), 0).astype(F32)
    iota_b = iota_f.astype(BF16)
    iota_b4 = jnp.concatenate([iota_b] * 4, axis=1)
    iota_f4 = jnp.concatenate([iota_f] * 4, axis=1)

    @pl.loop(0, 16)
    def _(k):
        lo = lo_ref[pl.ds(k, 1), :].astype(BF16)
        lot[k] = jnp.where(iota_b4 == lo, jnp.bfloat16(1), jnp.bfloat16(0))

    def spread(z):
        acc[...] = jnp.zeros_like(acc)

        @pl.loop(0, 16)
        def _(k):
            hit = iota_b4 == hi_ref[pl.ds(k, 1), :].astype(BF16)
            z_hi, z_lo = pieces(w_ref[pl.ds(k, 1), :] * z)
            zero = jnp.bfloat16(0)
            lhs = jnp.concatenate([jnp.where(hit, z_hi, zero), jnp.where(hit, z_lo, zero)], axis=0)
            acc[...] += lax.dot_general(lhs, lot[k], NT, preferred_element_type=F32)

        return acc[0:256, :] + acc[256:512, :]

    def observe(field):
        g_hi, g_lo = pieces(field)
        g2[0:256, :] = g_hi
        g2[256:512, :] = g_lo

        def step(k, total):
            t = dot(g2[...], lot[k])
            hit = iota_f4 == hi_ref[pl.ds(k, 1), :]
            found = jnp.where(hit, t[0:256] + t[256:512], 0.0)
            return total + w_ref[pl.ds(k, 1), :] * jnp.sum(found.reshape(32, 8, 512), axis=0)

        total = lax.fori_loop(0, 16, step, jnp.zeros((8, 512), F32))
        return jnp.sum(total, axis=0, keepdims=True)

    edge_low = lax.broadcasted_iota(I32, (256, 128), 1) < 64

    def along_y(g, ref):
        blank = jnp.zeros((32, 128), F32)
        up = jnp.concatenate([g[32:, 0:128], blank], axis=0)
        down = jnp.concatenate([blank, g[:224, 128:256]], axis=0)
        full = jnp.concatenate([g, jnp.where(edge_low, up, down)], axis=1)
        hi, lo = pieces(full)
        t_hi, t_lo = ref[0:384, :], ref[384:768, :]
        return dot(hi, t_hi) + dot(lo, t_hi) + dot(hi, t_lo)

    def halo(n, z):
        fown[n] = along_y(std[...] * spread(z), tyt)
        both = []
        for side, (to, dst) in enumerate(((left, fr), (right, fl))):
            both.append(
                pltpu.make_async_remote_copy(
                    src_ref=fown.at[n],
                    dst_ref=dst.at[n],
                    send_sem=hsem_s.at[n, side],
                    recv_sem=hsem_r.at[n, side],
                    device_id=(to, lev),
                    device_id_type=MESH,
                )
            )
            both[-1].start()
        for copy in both:
            copy.wait()

    def along_x(n, out):
        for t in range(8):
            rows = slice(t * 32, t * 32 + 32)
            window = jnp.concatenate([fl[n, rows, :], fown[n, rows, :], fr[n, rows, :]], axis=0)
            hi, lo = pieces(window)
            r1 = dot(ax_ref[...], hi)
            r = r1[0:64] + r1[64:128] + dot(ax_ref[0:64, :], lo)
            out[rows, :] = r[0:32]
            vbuf[rows, :] = r[32:64]

    halo(0, wd)
    along_x(0, bbuf)
    bb_f[...] = std[...] * along_y(vbuf[...], ty)
    y0 = observe(bb_f[...])
    halo(1, wgt * y0)
    along_x(1, ubuf)

    for g in range(2):
        for h in range(2):
            x = []
            for buf in (bbuf, ubuf):
                turned = buf[g * 128 : g * 128 + 128, h * 128 : h * 128 + 128].T
                turned = turned.reshape(8, 16, 128)
                x += [turned[:, 0:8, :], turned[:, 8:16, :]]
            for t, m in enumerate(lane_blocks(x)):
                at = ((4 * g + t) * 16 + h * 8) * 8
                xsend[at : at + 64, :] = m.reshape(64, 128)

    own2 = pltpu.make_async_copy(xsend.at[pl.ds(me * 8, 8)], xrecv.at[pl.ds(me * 8, 8)], lsem.at[1])
    own2.start()

    def turn_copy(q, n=1):
        return pltpu.make_async_remote_copy(
            src_ref=xsend.at[pl.ds(q * 8, 8 * n)],
            dst_ref=xrecv.at[pl.ds((me if n == 1 else 0) * 8, 8 * n)],
            send_sem=xsem.at[0],
            recv_sem=xsem.at[1],
            device_id=(q if n == 1 else right, lev),
            device_id_type=MESH,
        )

    @pl.loop(1, PENCILS)
    def _(i):
        turn_copy(lax.rem(me + i, PENCILS)).start()

    bu_f[...] = std[...] * along_y(vbuf[...], ty)
    y1 = observe(bu_f[...])

    def fold(v):
        return jnp.sum(v.reshape(32, 8, 256), axis=0)

    def cells_row(p):
        p = fold(p)
        return jnp.sum(p[:, 0:128] + p[:, 128:256], axis=0, keepdims=True)

    def obs_row(p):
        return p[:, 0:128] + p[:, 128:256] + p[:, 256:384] + p[:, 384:512]

    b, u = bbuf[...], ubuf[...]
    rows6 = [
        cells_row(b * b), cells_row(b * u), cells_row(u * u),
        obs_row(wgt * y0 * y0), obs_row(wgt * y0 * y1), obs_row(wgt * y1 * y1),
    ]
    sub = lax.broadcasted_iota(I32, (8, 128), 0)
    stack = jnp.zeros((8, 128), F32)
    for i, r in enumerate(rows6):
        stack = jnp.where(sub == i, r, stack)
    sums = jnp.sum(stack, axis=1, keepdims=True)
    diagonal = sub == lax.broadcasted_iota(I32, (8, 128), 1)
    local = jnp.sum(jnp.where(diagonal, sums, 0.0), axis=0, keepdims=True)

    def sum_over(mine, n, count, send, recv, sem, target):
        send[0] = mine
        recv[n] = mine

        def copy(i, many=False):
            return pltpu.make_async_remote_copy(
                src_ref=recv.at[pl.ds(0, count - 1)] if many else send.at[pl.ds(0, 1)],
                dst_ref=recv.at[pl.ds(0, count - 1)] if many else recv.at[pl.ds(n, 1)],
                send_sem=sem.at[0],
                recv_sem=sem.at[1],
                device_id=target(i),
                device_id_type=MESH,
            )

        @pl.loop(1, count)
        def _(i):
            copy(lax.rem(n + i, count)).start()

        done = copy(0, True)
        done.wait_send()
        done.wait_recv()
        total = recv[0]
        for i in range(1, count):
            total = total + recv[i]
        return total

    total = sum_over(local, near, NEAR, asend, arecv, asem, lambda i: (row * NEAR + i, lev))
    total = sum_over(
        total, row * LEVS + lev, FAR_Y * LEVS, csend, crecv, csem,
        lambda i: (lax.div(i, LEVS) * NEAR + near, lax.rem(i, LEVS)),
    )
    bb, bu, uu, q00, q01, q11 = [total[:, i : i + 1] for i in range(6)]

    ratio = bu / bb
    alpha0 = 1.0 / (1.0 + ratio)
    norm1 = alpha0 * alpha0 * (uu - ratio * bu)
    gb = ratio * alpha0 + norm1 / bb
    gu = -alpha0
    curve = gb * gb * (bb + q00) + 2.0 * gb * gu * (bu + q01) + gu * gu * (uu + q11)
    alpha1 = norm1 / curve
    c_b = alpha0 + alpha1 * gb
    c_u = alpha1 * gu

    for t in range(8):
        rows = slice(t * 32, t * 32 + 32)
        incr_out[0, :, t * 256 : t * 256 + 256] = c_b * bb_f[rows, :] + c_u * bu_f[rows, :]

    own2.wait()
    turned = turn_copy(0, PENCILS - 1)
    turned.wait_send()
    turned.wait_recv()
    got = xrecv[...].reshape(32, 4, 8, 128)
    parts = lane_blocks([got[:, i] for i in range(4)])
    for rh in range(2):
        value = c_b * parts[rh] + c_u * parts[2 + rh]
        for p in range(32):
            control_out[0, rh * 8 : rh * 8 + 8, p * 128 : p * 128 + 128] = value[p]


def body(background_std, x_kernel, y_kernel, obs_owner, obs_cells, obs_weights, innovation, obs_precision, obs_counts):
    holding = obs_owner.shape[0]
    vmem = pl.BlockSpec(memory_space=pltpu.VMEM)
    smem = pl.BlockSpec(memory_space=pltpu.SMEM)
    field = pltpu.VMEM((256, 256), F32)
    dma = pltpu.SemaphoreType.DMA
    return pl.pallas_call(
        kernel,
        out_shape=(
            jax.ShapeDtypeStruct((1, 16, 4096), F32),
            jax.ShapeDtypeStruct((1, 32, 2048), F32),
        ),
        in_specs=[vmem, smem, smem, vmem, vmem, vmem, vmem, vmem, smem],
        out_specs=(vmem, vmem),
        scratch_shapes=[
            pltpu.VMEM((256, 128), F32), pltpu.VMEM((256, 128), F32),
            pltpu.VMEM((256, 128), F32),
            pltpu.VMEM((16, 512), F32), pltpu.VMEM((16, 512), F32), pltpu.VMEM((16, 512), F32),
            pltpu.VMEM((16, 256, 512), BF16),
            pltpu.VMEM((768, 256), BF16), pltpu.VMEM((768, 256), BF16),
            pltpu.VMEM((128, 96), BF16),
            field,
            pltpu.VMEM((512, 256), BF16),
            pltpu.VMEM((512, 256), F32),
            pltpu.VMEM((2, 256, 256), F32), pltpu.VMEM((2, 256, 256), F32), pltpu.VMEM((2, 256, 256), F32),
            field, field, field, field, field,
            pltpu.VMEM((1024, 128), F32), pltpu.VMEM((1024, 128), F32),
            pltpu.VMEM((1, 1, 128), F32), pltpu.VMEM((NEAR, 1, 128), F32),
            pltpu.VMEM((1, 1, 128), F32), pltpu.VMEM((FAR_Y * LEVS, 1, 128), F32),
            dma((2,)), dma((2, 2)), dma((2, 2)), dma((2,)), dma((2,)), dma((2,)), dma((2,)),
        ],
        compiler_params=pltpu.CompilerParams(
            collective_id=0, has_side_effects=True, vmem_limit_bytes=48 << 20
        ),
        name="assimilate",
    )(
        background_std, x_kernel, y_kernel, obs_owner.reshape(1, holding), obs_cells.T, obs_weights.T,
        innovation.reshape(1, holding), obs_precision.reshape(1, holding), obs_counts,
    )


def solution(mesh):
    return jax.shard_map(
        body,
        mesh=mesh,
        in_specs=(
            P("lev", "pencil", None),
            P("lev", None),
            P("lev", None),
            P(("pencil", "lev"), None),
            P(("pencil", "lev"), None),
            P(("pencil", "lev"), None),
            P(("pencil", "lev")),
            P(("pencil", "lev")),
            P(("pencil", "lev")),
        ),
        out_specs=(P("lev", "pencil", None), P("lev", "pencil", None)),
        check_vma=False,
    )
```

time: 1140 us -> 85.5 us (0.07)
  other arithmetic: 504 us -> 0 us
  blocking collectives: 381 us -> 0 us
  local copies, waits for them, and re-layouts: 152 us -> 4.48 us
  Pallas kernels: 0 us -> 79.4 us
  waiting for transfers between devices: 48.3 us -> 0 us
  starting transfers between devices: 42.4 us -> 0 us
    psum x3 -> x0, blocking collectives: 286 us -> none  [the longest x2 191 us: total_squares(): return lax.psum(jnp.sum(values * values), ('pencil', 'lev'))]
    scatter-add x3 -> x0, other arithmetic: 146 us -> none  [spread(): total.at[stencil.reshape(-1)].add((interp * values[:, None]).reshape(-1))]
    unnamed x8 -> x0, other arithmetic: 129 us -> none
    all_to_all x4 -> x0, blocking collectives: 94.6 us -> none  [the longest x2 47.7 us: forward(): lax.all_to_all(along_x, 'pencil', split_axis=2, concat_axis=1, tiled=True)]
    gather x4 -> x0, local copies, waits for them, and re-layouts: 91.3 us -> none  [body(): smoothed.reshape(-1)[stencil]]
    add x6 -> x0, other arithmetic: 85.9 us -> none  [the longest x4 85.8 us: smooth(): result + kernel_taps[:, offset][:, None, None] * padded[:, :, offset:offs...]
    pallas_call x0 -> x1, Pallas kernels: none -> 79.4 us  [body(): pl.pallas_call(kernel, out_shape=(jax.ShapeDtypeStruct((1, 16, 4096), F32...]
    transpose x3 -> x0, other arithmetic: 63.9 us -> none  [adjoint(): jnp.swapaxes(along_y, 1, 2)]
  transfers between devices with their start and end apart: 4 -> 0, of which waited for: 4 -> 0; matrix products, arithmetic and copies ran while one was open for 1% -> 0% of each run, Pallas kernels for 0% -> 0%
where the time goes in v1:
time: 85.5 us; the launch traced here: 85.2 us
  Pallas kernels  79.4 us (93%)
  local copies, waits for them, and re-layouts  4.48 us (5%)
  between operations  1.33 us (2%)
    pallas_call x1, Pallas kernels, body(): pl.pallas_call(kernel, out_shape=(jax.ShapeDtypeStruct((1, 16, 4096), F32...  79.4 us
    unnamed x18, local copies, waits for them, and re-layouts  4.48 us

profile of v1, /device:TPU:1, one launch (start us, length us, event | category | flops | bytes accessed | tf_op | source)
XLA Modules:
  0.0 85.2 jit_solution(13034640348590678056)
XLA Ops:
  1.3 0.0 copy-start.7
  1.3 0.0 copy-start.4
  1.3 0.0 copy-start.5
  1.3 0.0 copy-start.3
  1.3 0.0 copy-start.6
  1.3 0.6 copy-done.7
  1.9 0.0 copy-done.4
  2.0 0.0 copy-done.5
  2.0 0.0 copy-done.3
  2.0 0.0 copy-done.6
  2.0 0.0 copy-start
  2.0 0.9 %copy-done = f32[1,32,2048]{2,1,0:T(8,128)S(1)} copy-done((f32[1,32,2048]{2,1,0:T(8,128)S(1)}, f32[1,32,2048]{2,1,0:T(8,128)}, u32[]{:S(2)}) %copy-start) | copy-done | bytes 262168
  3.0 0.0 copy-start.1
  3.0 0.7 copy-done.1
  3.7 0.0 copy-start.2
  3.7 0.7 copy-done.2
  4.4 79.4 %assimilate.1 = (f32[1,16,4096]{2,1,0:T(8,128)S(1)}, f32[1,32,2048]{2,1,0:T(8,128)S(1)}) custom-call(f32[1,32,2048]{2,1,0:T(8,128)S(1)} %copy-done, f32[1,31]{1,0:T(1,128)S(1)} %copy-done.6, f32[1,31]{1,0:T(1,128)S(1)} %copy-done.7, s32[1,256]{1,0:T(1,128)S(1)} %bitcast.7, s32[16,256]{1,0:T(8,128)S(1)} %bitcast.5, f32[16,256]{1,0:T(8,128)S(1)} %bitcast.6, ...), custom_call_target="tpu_custom_call" | custom-call | tf_op jit(solution)/shard_map/assimilate/pallas_call | solution.py:370
  83.8 0.7 copy.14
  84.5 0.7 copy.15
Async XLA Ops:
  1.3 0.7 copy-start.7
  1.3 0.7 copy-start.4
  1.3 0.7 copy-start.5
  1.3 0.7 copy-start.3
  1.3 0.7 copy-start.6
  2.0 1.0 %copy-start = (f32[1,32,2048]{2,1,0:T(8,128)S(1)}, f32[1,32,2048]{2,1,0:T(8,128)}, u32[]{:S(2)}) copy-start(f32[1,32,2048]{2,1,0:T(8,128)} %std_in.1) | copy-start | bytes 786436
  3.0 0.7 copy-start.1
  3.7 0.7 copy-start.2

commit v2 on v1

v2 whole, which is shorter than its diff:
```python
import functools

import jax
import jax.numpy as jnp
from jax import lax
from jax.experimental import pallas as pl
from jax.experimental.pallas import tpu as pltpu
from jax.sharding import PartitionSpec as P

F32, BF16, I32 = jnp.float32, jnp.bfloat16, jnp.int32
MESH = pl.DeviceIdType.MESH
HALF = 15
PENCILS = 128
LEVS = 4
NEAR = 16
FAR_Y = 8
SLOTS = 4
NT = (((1,), (1,)), ((), ()))
FARTHEST = (8, 7, 9, 6, 10, 5, 11, 4, 12, 3, 13, 2, 14, 1, 15, 0)
CHUNKS = 2
PART = 256 // CHUNKS


def dot(a, b):
    return jnp.dot(a, b, preferred_element_type=F32)


def pieces(v):
    hi = v.astype(BF16)
    return hi, (v - hi.astype(F32)).astype(BF16)


def band(delta, taps, sign):
    out = jnp.zeros(delta.shape, F32)
    for d in range(-HALF, HALF + 1):
        out = jnp.where(delta == d, taps[0, HALF + sign * d], out)
    return out


def lane_blocks(x):
    lane = lax.broadcasted_iota(I32, x[0].shape, x[0].ndim - 1)
    ax = x[0].ndim - 1
    low, even = lane < 64, (lane & 32) == 0

    def halves(a, b):
        return jnp.where(low, a, pltpu.roll(b, 64, ax)), jnp.where(low, pltpu.roll(a, 64, ax), b)

    def quarters(a, b):
        return jnp.where(even, a, pltpu.roll(b, 32, ax)), jnp.where(even, pltpu.roll(a, 96, ax), b)

    a, c = halves(x[0], x[2])
    b, d = halves(x[1], x[3])
    return quarters(a, b) + quarters(c, d)


def kernel(
    std_hbm, xk_hbm, yk_hbm, owner_hbm, cells_hbm, weights_hbm, innov_hbm, prec_hbm, counts_hbm,
    control_out, incr_out,
    std_in, xk, yk, owner, cells, weights, innov, prec, counts,
    osend, orecv, rt_ref, hi_ref, lo_ref, w_ref, lot,
    ty, tyt, ax_ref, std, g2, acc,
    fown, fl, fr, vbuf, bbuf, ubuf, bb_f, bu_f,
    turned, ctl, xsend, xrecv, asend, arecv, csend, crecv,
    isem, osem, hsem_s, hsem_r, xsem, asem, csem, lsem,
):
    me = lax.axis_index("pencil")
    lev = lax.axis_index("lev")
    near = lax.rem(me, NEAR)
    row = lax.div(me, NEAR)
    left, right = lax.rem(me + PENCILS - 1, PENCILS), lax.rem(me + 1, PENCILS)
    zcs = [lax.rem(near + j, NEAR) for j in FARTHEST]

    def peer_row(i):
        dy = FAR_Y // 2 + lax.div(i + 1, 2) * (1 - 2 * lax.rem(i, 2))
        return lax.rem(row + dy, FAR_Y) * NEAR

    def each_peer(act):
        @pl.loop(0, FAR_Y - 1)
        def _(i):
            base = peer_row(i)
            for zc in zcs:
                act(base + zc)

        for zc in zcs[:-1]:
            act(row * NEAR + zc)

    loads = [
        pltpu.make_async_copy(src, dst, isem.at[i])
        for i, (src, dst) in enumerate(
            (
                (owner_hbm, owner), (prec_hbm, prec), (innov_hbm, innov), (counts_hbm, counts),
                (cells_hbm, cells), (weights_hbm, weights), (xk_hbm, xk), (yk_hbm, yk), (std_hbm, std_in),
            )
        )
    ]
    for load in loads:
        load.start()
    barrier = pltpu.get_barrier_semaphore()

    def hello(q, to_lev=lev):
        pl.semaphore_signal(barrier, inc=1, device_id=(q, to_lev), device_id_type=MESH)

    each_peer(hello)

    @pl.loop(0, FAR_Y)
    def _(i):
        for dx in (2, 1, 3):
            hello(lax.rem(row + FAR_Y // 2 + i, FAR_Y) * NEAR + near, lax.rem(lev + dx, LEVS))

    for load in loads[:6]:
        load.wait()

    n_obs = cells.shape[1]
    lane_o = lax.broadcasted_iota(I32, (1, n_obs), 1)
    weight = jnp.where(lane_o < counts[0, 0], prec[...], 0.0)
    member = lax.broadcasted_iota(I32, (PENCILS, n_obs), 0) == owner[...]
    member_b = jnp.where(member, 1.0, 0.0).astype(BF16)
    before = lax.broadcasted_iota(I32, (n_obs, n_obs), 0) < lax.broadcasted_iota(I32, (n_obs, n_obs), 1)
    rank = dot(member_b, jnp.where(before, 1.0, 0.0).astype(BF16))
    sub8 = lax.broadcasted_iota(I32, (8, n_obs), 0)
    tail = jnp.where(sub8 == 0, weight * innov[...], jnp.where(sub8 == 1, weight, 0.0))
    feats = jnp.concatenate(
        [cells[...].astype(F32), weights[...], tail, jnp.zeros((24, n_obs), F32)], axis=0
    )
    f0 = feats.astype(BF16)
    rest = feats - f0.astype(F32)
    f1 = rest.astype(BF16)
    f2 = (rest - f1.astype(F32)).astype(BF16)
    packed = []
    for s in range(SLOTS):
        pick = jnp.where(member, jnp.where(rank == float(s), 1.0, 0.0), 0.0).astype(BF16)
        parts = [lax.dot_general(pick, f, NT, preferred_element_type=F32) for f in (f0, f1, f2)]
        packed.append(parts[0] + parts[1] + parts[2])
    for h in range(2):
        osend[pl.ds(h, PENCILS, stride=2), :] = jnp.concatenate(packed[2 * h : 2 * h + 2], axis=1)

    pl.semaphore_wait(barrier, PENCILS - 1 + FAR_Y * (LEVS - 1))

    own = pltpu.make_async_copy(osend.at[pl.ds(me * 2, 2)], orecv.at[pl.ds(me * 2, 2)], lsem.at[0])
    own.start()

    def obs_copy(q, n=1):
        return pltpu.make_async_remote_copy(
            src_ref=osend.at[pl.ds(q * 2, 2 * n)],
            dst_ref=orecv.at[pl.ds((me if n == 1 else 0) * 2, 2 * n)],
            send_sem=osem.at[0],
            recv_sem=osem.at[1],
            device_id=(q if n == 1 else right, lev),
            device_id_type=MESH,
        )

    each_peer(lambda q: obs_copy(q).start())
    for load in loads[6:]:
        load.wait()

    base_delta = lax.broadcasted_iota(I32, (8, 512), 0) - lax.broadcasted_iota(I32, (8, 512), 1) + 256
    for sign, ref in ((1, ty), (-1, tyt)):
        base = band(base_delta, yk, sign)
        for g in range(48):
            p0 = 8 * g if g < 40 else 8 * g - 384
            r = pltpu.roll(base, (p0 - 256) % 512, 1)[:, :256]
            acc[8 * g : 8 * g + 8, :] = r
        hi, lo = pieces(acc[0:384, :])
        ref[0:384, :] = hi
        ref[384:768, :] = hi
        ref[768:1152, :] = lo
    delta = lax.broadcasted_iota(I32, (32, 96), 1) - lax.broadcasted_iota(I32, (32, 96), 0) - 32
    delta_w = lax.broadcasted_iota(I32, (96, 96), 1) - lax.broadcasted_iota(I32, (96, 96), 0)
    a1 = band(delta, xk, -1)
    a2 = jnp.dot(
        band(delta, xk, 1),
        band(delta_w, xk, -1),
        preferred_element_type=F32,
        precision=lax.Precision.HIGHEST,
    )
    a_hi, a_lo = pieces(jnp.concatenate([a1, a2], axis=0))
    ax_ref[0:64, :] = a_hi
    ax_ref[64:128, :] = a_lo
    for t in range(8):
        std[t * 32 : t * 32 + 32, :] = std_in[0, :, t * 256 : t * 256 + 256]

    own.wait()
    everyone = obs_copy(0, PENCILS - 1)
    everyone.wait_send()
    everyone.wait_recv()

    for h in range(2):
        rt_ref[h * 128 : h * 128 + 128, :] = orecv[pl.ds(h, PENCILS, stride=2), :].T
    wd, wgt = [], []
    for s in range(SLOTS):
        c = rt_ref[s * 64 : s * 64 + 16, :].astype(I32)
        cols = slice(s * 128, s * 128 + 128)
        hi_ref[:, cols] = (((c >> 8) & 7) * 32 + (c >> 11)).astype(F32)
        lo_ref[:, cols] = (c & 255).astype(F32)
        w_ref[:, cols] = rt_ref[s * 64 + 16 : s * 64 + 32, :]
        wd.append(rt_ref[s * 64 + 32 : s * 64 + 33, :])
        wgt.append(rt_ref[s * 64 + 33 : s * 64 + 34, :])
    wd, wgt = jnp.concatenate(wd, axis=1), jnp.concatenate(wgt, axis=1)
    iota_f = lax.broadcasted_iota(I32, (256, 128), 0).astype(F32)
    iota_b = iota_f.astype(BF16)
    iota_b4 = jnp.concatenate([iota_b] * 4, axis=1)
    iota_f4 = jnp.concatenate([iota_f] * 4, axis=1)
    one, zero = jnp.bfloat16(1), jnp.bfloat16(0)

    def spread(z, first):
        acc[...] = jnp.zeros_like(acc)

        @pl.loop(0, 4)
        def _(n):
            lhs = []
            for j in range(4):
                k = n * 4 + j
                if first:
                    lo = lo_ref[pl.ds(k, 1), :].astype(BF16)
                    lot[n, :, j * 512 : j * 512 + 512] = jnp.where(iota_b4 == lo, one, zero)
                hit = iota_b4 == hi_ref[pl.ds(k, 1), :].astype(BF16)
                z_hi, z_lo = pieces(w_ref[pl.ds(k, 1), :] * z)
                lhs.append(jnp.concatenate([jnp.where(hit, z_hi, zero), jnp.where(hit, z_lo, zero)], axis=0))
            acc[...] += lax.dot_general(jnp.concatenate(lhs, axis=1), lot[n], NT, preferred_element_type=F32)

        return acc[0:256, :] + acc[256:512, :]

    def observe(field, send):
        g_hi, g_lo = pieces(field)
        g2[0:256, :] = g_hi
        g2[256:512, :] = g_lo
        for i in (1, 3, 5):
            send(peer_row(i) + zcs[-1])

        def step(n, total):
            first, second = peer_row(2 * n), peer_row(2 * n + 1)
            for zc in zcs:
                send(first + zc)
            for zc in zcs[:-1]:
                send(second + zc)
            both = dot(g2[...], lot[n])
            for j in range(4):
                k = n * 4 + j
                t = both[:, j * 512 : j * 512 + 512]
                found = jnp.where(iota_f4 == hi_ref[pl.ds(k, 1), :], t[0:256] + t[256:512], 0.0)
                total += w_ref[pl.ds(k, 1), :] * jnp.sum(found.reshape(32, 8, 512), axis=0)
            return total

        total = lax.fori_loop(0, 4, step, jnp.zeros((8, 512), F32))
        return jnp.sum(total, axis=0, keepdims=True)

    edge_low = lax.broadcasted_iota(I32, (256, 128), 1) < 64

    def y_operand(g):
        blank = jnp.zeros((32, 128), F32)
        up = jnp.concatenate([g[32:, 0:128], blank], axis=0)
        down = jnp.concatenate([blank, g[:224, 128:256]], axis=0)
        hi, lo = pieces(jnp.concatenate([g, jnp.where(edge_low, up, down)], axis=1))
        return jnp.concatenate([hi, lo, hi], axis=1)

    def halo(n, z):
        operand = y_operand(std[...] * spread(z, n == 0))
        copies = []
        for c in range(CHUNKS):
            rows = slice(c * PART, c * PART + PART)
            fown[n, rows, :] = dot(operand[rows], tyt[...])
            both = []
            for side, (to, dst) in enumerate(((left, fr), (right, fl))):
                both.append(
                    pltpu.make_async_remote_copy(
                        src_ref=fown.at[n, pl.ds(c * PART, PART)],
                        dst_ref=dst.at[n, pl.ds(c * PART, PART)],
                        send_sem=hsem_s.at[n, side, c],
                        recv_sem=hsem_r.at[n, side, c],
                        device_id=(to, lev),
                        device_id_type=MESH,
                    )
                )
                both[-1].start()
            copies.append(both)
        return copies

    def along_x(n, copies, out):
        for c in range(CHUNKS):
            for copy in copies[c]:
                copy.wait_recv()
            for t in range(c * 8 // CHUNKS, (c + 1) * 8 // CHUNKS):
                rows = slice(t * 32, t * 32 + 32)
                window = jnp.concatenate([fl[n, rows, :], fown[n, rows, :], fr[n, rows, :]], axis=0)
                hi, lo = pieces(window)
                r1 = dot(ax_ref[...], hi)
                r = r1[0:64] + r1[64:128] + dot(ax_ref[0:64, :], lo)
                out[rows, :] = r[0:32]
                vbuf[rows, :] = r[32:64]

    pp, p4 = lax.rem(me, 4), lax.div(me, 4) * 4

    def turn(f, buf):
        for g in range(2):
            for h in range(2):
                turned[...] = buf[g * 128 : g * 128 + 128, h * 128 : h * 128 + 128].T
                x = [turned[pl.ds(i, 32, stride=4), :] for i in range(4)]
                for t, m in enumerate(lane_blocks(x)):
                    at = ((4 * g + t) * 16 + h * 8) * 4
                    xsend[f, at : at + 32, :] = m
        mine = pltpu.make_async_copy(
            xsend.at[f, pl.ds(me * 4, 4)], xrecv.at[f, pp, pl.ds(p4, 4)], lsem.at[1 + f]
        )
        mine.start()
        return mine

    def turn_copy(f, q):
        return pltpu.make_async_remote_copy(
            src_ref=xsend.at[f, pl.ds(q * 4, 4)],
            dst_ref=xrecv.at[f, pp, pl.ds(p4, 4)],
            send_sem=xsem.at[0, f],
            recv_sem=xsem.at[1, f],
            device_id=(q, lev),
            device_id_type=MESH,
        )

    def turn_wait(f, mine):
        mine.wait()
        every = xsend.at[f, pl.ds(0, 4 * (PENCILS - 1))]
        whole = pltpu.make_async_remote_copy(
            src_ref=every,
            dst_ref=every,
            send_sem=xsem.at[0, f],
            recv_sem=xsem.at[1, f],
            device_id=(right, lev),
            device_id_type=MESH,
        )
        whole.wait_send()
        whole.wait_recv()

    hops0 = halo(0, wd)
    along_x(0, hops0, bbuf)
    bb_f[...] = std[...] * dot(y_operand(vbuf[...]), ty[...])
    own_b = turn(0, bbuf)
    y0 = observe(bb_f[...], lambda q: turn_copy(0, q).start())
    hops1 = halo(1, wgt * y0)
    along_x(1, hops1, ubuf)
    own_u = turn(1, ubuf)
    bu_f[...] = std[...] * dot(y_operand(vbuf[...]), ty[...])
    y1 = observe(bu_f[...], lambda q: turn_copy(1, q).start())

    def fold(v):
        return jnp.sum(v.reshape(32, 8, 256), axis=0)

    def cells_row(p):
        p = fold(p)
        return jnp.sum(p[:, 0:128] + p[:, 128:256], axis=0, keepdims=True)

    def obs_row(p):
        return p[:, 0:128] + p[:, 128:256] + p[:, 256:384] + p[:, 384:512]

    b, u = bbuf[...], ubuf[...]
    rows6 = [
        cells_row(b * b), cells_row(b * u), cells_row(u * u),
        obs_row(wgt * y0 * y0), obs_row(wgt * y0 * y1), obs_row(wgt * y1 * y1),
    ]
    sub = lax.broadcasted_iota(I32, (8, 128), 0)
    stack = jnp.zeros((8, 128), F32)
    for i, r in enumerate(rows6):
        stack = jnp.where(sub == i, r, stack)
    sums = jnp.sum(stack, axis=1, keepdims=True)
    diagonal = sub == lax.broadcasted_iota(I32, (8, 128), 1)
    local = jnp.sum(jnp.where(diagonal, sums, 0.0), axis=0, keepdims=True)

    def sum_over(mine, n, count, send, recv, sem, targets):
        send[0] = mine
        recv[n] = mine

        def copy(to, many=False):
            return pltpu.make_async_remote_copy(
                src_ref=recv.at[pl.ds(0, count - 1)] if many else send.at[pl.ds(0, 1)],
                dst_ref=recv.at[pl.ds(0, count - 1)] if many else recv.at[pl.ds(n, 1)],
                send_sem=sem.at[0],
                recv_sem=sem.at[1],
                device_id=to,
                device_id_type=MESH,
            )

        for to in targets:
            copy(to).start()
        done = copy(targets[0], True)
        done.wait_send()
        done.wait_recv()
        parts = [recv[i] for i in range(count)]
        while len(parts) > 1:
            parts = [parts[i] + parts[i + 1] for i in range(0, len(parts), 2)]
        return parts[0]

    total = sum_over(local, near, NEAR, asend, arecv, asem, [(row * NEAR + zc, lev) for zc in zcs[:-1]])
    total = sum_over(
        total, row * LEVS + lev, FAR_Y * LEVS, csend, crecv, csem,
        [
            (lax.rem(row + dy, FAR_Y) * NEAR + near, lax.rem(lev + dx, LEVS))
            for dy in (4, 3, 5, 2, 6, 1, 7, 0)
            for dx in (2, 1, 3, 0)
            if dx or dy
        ],
    )
    bb, bu, uu, q00, q01, q11 = [total[:, i : i + 1] for i in range(6)]

    ratio = bu / bb
    alpha0 = 1.0 / (1.0 + ratio)
    norm1 = alpha0 * alpha0 * (uu - ratio * bu)
    gb = ratio * alpha0 + norm1 / bb
    gu = -alpha0
    curve = gb * gb * (bb + q00) + 2.0 * gb * gu * (bu + q01) + gu * gu * (uu + q11)
    alpha1 = norm1 / curve
    c_b = alpha0 + alpha1 * gb
    c_u = alpha1 * gu

    for t in range(8):
        rows = slice(t * 32, t * 32 + 32)
        incr_out[0, :, t * 256 : t * 256 + 256] = c_b * bb_f[rows, :] + c_u * bu_f[rows, :]

    for copies in hops0 + hops1:
        for copy in copies:
            copy.wait_send()
    turn_wait(0, own_b)
    turn_wait(1, own_u)
    got_b = lane_blocks([xrecv[0, i] for i in range(4)])
    got_u = lane_blocks([xrecv[1, i] for i in range(4)])
    for i in range(4):
        ctl[pl.ds(i, 128, stride=4), :] = c_b * got_b[i] + c_u * got_u[i]
    for p in range(32):
        control_out[0, :, p * 128 : p * 128 + 128] = ctl[p * 16 : p * 16 + 16, :]


def body(background_std, x_kernel, y_kernel, obs_owner, obs_cells, obs_weights, innovation, obs_precision, obs_counts):
    holding = obs_owner.shape[0]
    vmem = pl.BlockSpec(memory_space=pltpu.VMEM)
    hbm = pl.BlockSpec(memory_space=pltpu.HBM)
    field = pltpu.VMEM((256, 256), F32)
    dma = pltpu.SemaphoreType.DMA
    keep = lambda x: pltpu.with_memory_space_constraint(x, pltpu.HBM)
    return pl.pallas_call(
        kernel,
        out_shape=(
            jax.ShapeDtypeStruct((1, 16, 4096), F32),
            jax.ShapeDtypeStruct((1, 32, 2048), F32),
        ),
        in_specs=[hbm] * 9,
        out_specs=(vmem, vmem),
        scratch_shapes=[
            pltpu.VMEM((1, 32, 2048), F32), pltpu.SMEM((1, 31), F32), pltpu.SMEM((1, 31), F32),
            pltpu.VMEM((1, holding), I32), pltpu.VMEM((16, holding), I32), pltpu.VMEM((16, holding), F32),
            pltpu.VMEM((1, holding), F32), pltpu.VMEM((1, holding), F32), pltpu.SMEM((1, 1), I32),
            pltpu.VMEM((256, 128), F32), pltpu.VMEM((256, 128), F32),
            pltpu.VMEM((256, 128), F32),
            pltpu.VMEM((16, 512), F32), pltpu.VMEM((16, 512), F32), pltpu.VMEM((16, 512), F32),
            pltpu.VMEM((4, 256, 2048), BF16),
            pltpu.VMEM((1152, 256), BF16), pltpu.VMEM((1152, 256), BF16),
            pltpu.VMEM((128, 96), BF16),
            field,
            pltpu.VMEM((512, 256), BF16),
            pltpu.VMEM((512, 256), F32),
            pltpu.VMEM((2, 256, 256), F32), pltpu.VMEM((2, 256, 256), F32), pltpu.VMEM((2, 256, 256), F32),
            field, field, field, field, field,
            pltpu.VMEM((128, 128), F32), pltpu.VMEM((512, 128), F32),
            pltpu.VMEM((2, 512, 128), F32), pltpu.VMEM((2, 4, 128, 128), F32),
            pltpu.VMEM((1, 1, 128), F32), pltpu.VMEM((NEAR, 1, 128), F32),
            pltpu.VMEM((1, 1, 128), F32), pltpu.VMEM((FAR_Y * LEVS, 1, 128), F32),
            dma((9,)), dma((2,)), dma((2, 2, CHUNKS)), dma((2, 2, CHUNKS)), dma((2, 2)), dma((2,)), dma((2,)), dma((3,)),
        ],
        compiler_params=pltpu.CompilerParams(
            collective_id=0, has_side_effects=True, vmem_limit_bytes=52 << 20
        ),
        name="assimilate",
    )(
        *map(keep, (background_std, x_kernel, y_kernel, obs_owner.reshape(1, holding), obs_cells.T, obs_weights.T,
        innovation.reshape(1, holding), obs_precision.reshape(1, holding))), obs_counts.reshape(1, 1),
    )


def solution(mesh):
    return jax.shard_map(
        body,
        mesh=mesh,
        in_specs=(
            P("lev", "pencil", None),
            P("lev", None),
            P("lev", None),
            P(("pencil", "lev"), None),
            P(("pencil", "lev"), None),
            P(("pencil", "lev"), None),
            P(("pencil", "lev")),
            P(("pencil", "lev")),
            P(("pencil", "lev")),
        ),
        out_specs=(P("lev", "pencil", None), P("lev", "pencil", None)),
        check_vma=False,
    )
```

time: 85.5 us -> 68.7 us (0.80)
  Pallas kernels: 79.4 us -> 65.9 us
  local copies, waits for them, and re-layouts: 4.48 us -> 1.41 us
    pallas_call x1, Pallas kernels: 79.4 us -> 65.9 us  [body(): pl.pallas_call(kernel, out_shape=(jax.ShapeDtypeStruct((1, 16, 4096), F32...]
    unnamed x18 -> x2, local copies, waits for them, and re-layouts: 4.48 us -> 1.41 us
where the time goes in v2:
time: 68.7 us; the launch traced here: 68.6 us
  Pallas kernels  65.9 us (96%)
  local copies, waits for them, and re-layouts  1.41 us (2%)
  between operations  1.29 us (2%)
    pallas_call x1, Pallas kernels, body(): pl.pallas_call(kernel, out_shape=(jax.ShapeDtypeStruct((1, 16, 4096), F32...  65.9 us
    unnamed x2, local copies, waits for them, and re-layouts  1.41 us

profile of v2, /device:TPU:1, one launch (start us, length us, event | category | flops | bytes accessed | tf_op | source)
XLA Modules:
  0.0 68.6 jit_solution(6301408980296214901)
XLA Ops:
  1.3 65.9 %assimilate.1 = (f32[1,16,4096]{2,1,0:T(8,128)S(1)}, f32[1,32,2048]{2,1,0:T(8,128)S(1)}) custom-call(f32[1,32,2048]{2,1,0:T(8,128)} %std_hbm.1, f32[1,31]{1,0:T(1,128)} %xk_hbm.1, f32[1,31]{1,0:T(1,128)} %yk_hbm.1, s32[1,256]{1,0:T(1,128)} %bitcast.9, s32[16,256]{1,0:T(8,128)} %bitcast.7, f32[16,256]{1,0:T(8,128)} %bitcast.8, f32[1,256]{1,0:T(1,128)} %bitcast.10, ...), custom_call_target="tpu_custom_call" | custom-call | tf_op jit(solution)/shard_map/assimilate/pallas_call | solution.py:435
  67.2 0.7 %copy.14 = f32[1,16,4096]{2,1,0:T(8,128)} copy(f32[1,16,4096]{2,1,0:T(8,128)S(1)} %get-tuple-element.4) | data formatting | bytes 524288
  67.9 0.7 %copy.15 = f32[1,32,2048]{2,1,0:T(8,128)} copy(f32[1,32,2048]{2,1,0:T(8,128)S(1)} %get-tuple-element.5) | data formatting | bytes 524288

commit v3 on v2

--- a/solution.py
+++ b/solution.py
@@ -220,19 +220,11 @@
 
         return acc[0:256, :] + acc[256:512, :]
 
-    def observe(field, send):
+    def observe(field):
         g_hi, g_lo = pieces(field)
         g2[0:256, :] = g_hi
         g2[256:512, :] = g_lo
-        for i in (1, 3, 5):
-            send(peer_row(i) + zcs[-1])
-
         def step(n, total):
-            first, second = peer_row(2 * n), peer_row(2 * n + 1)
-            for zc in zcs:
-                send(first + zc)
-            for zc in zcs[:-1]:
-                send(second + zc)
             both = dot(g2[...], lot[n])
             for j in range(4):
                 k = n * 4 + j
@@ -302,6 +294,7 @@
             xsend.at[f, pl.ds(me * 4, 4)], xrecv.at[f, pp, pl.ds(p4, 4)], lsem.at[1 + f]
         )
         mine.start()
+        each_peer(lambda q: turn_copy(f, q).start())
         return mine
 
     def turn_copy(f, q):
@@ -327,17 +320,18 @@
         )
         whole.wait_send()
         whole.wait_recv()
+        for i, m in enumerate(lane_blocks([xrecv[f, i] for i in range(4)])):
+            ctl[f, pl.ds(i, 128, stride=4), :] = m
 
     hops0 = halo(0, wd)
     along_x(0, hops0, bbuf)
     bb_f[...] = std[...] * dot(y_operand(vbuf[...]), ty[...])
     own_b = turn(0, bbuf)
-    y0 = observe(bb_f[...], lambda q: turn_copy(0, q).start())
+    y0 = observe(bb_f[...])
     hops1 = halo(1, wgt * y0)
     along_x(1, hops1, ubuf)
-    own_u = turn(1, ubuf)
     bu_f[...] = std[...] * dot(y_operand(vbuf[...]), ty[...])
-    y1 = observe(bu_f[...], lambda q: turn_copy(1, q).start())
+    y1 = observe(bu_f[...])
 
     def fold(v):
         return jnp.sum(v.reshape(32, 8, 256), axis=0)
@@ -362,7 +356,7 @@
     diagonal = sub == lax.broadcasted_iota(I32, (8, 128), 1)
     local = jnp.sum(jnp.where(diagonal, sums, 0.0), axis=0, keepdims=True)
 
-    def sum_over(mine, n, count, send, recv, sem, targets):
+    def sum_over(mine, n, count, send, recv, sem, targets, meanwhile=None):
         send[0] = mine
         recv[n] = mine
 
@@ -378,6 +372,8 @@
 
         for to in targets:
             copy(to).start()
+        if meanwhile:
+            meanwhile()
         done = copy(targets[0], True)
         done.wait_send()
         done.wait_recv()
@@ -386,7 +382,11 @@
             parts = [parts[i] + parts[i + 1] for i in range(0, len(parts), 2)]
         return parts[0]
 
-    total = sum_over(local, near, NEAR, asend, arecv, asem, [(row * NEAR + zc, lev) for zc in zcs[:-1]])
+    own_u = []
+    total = sum_over(
+        local, near, NEAR, asend, arecv, asem, [(row * NEAR + zc, lev) for zc in zcs[:-1]],
+        lambda: own_u.append(turn(1, ubuf)),
+    )
     total = sum_over(
         total, row * LEVS + lev, FAR_Y * LEVS, csend, crecv, csem,
         [
@@ -395,6 +395,7 @@
             for dx in (2, 1, 3, 0)
             if dx or dy
         ],
+        lambda: turn_wait(0, own_b),
     )
     bb, bu, uu, q00, q01, q11 = [total[:, i : i + 1] for i in range(6)]
 
@@ -415,14 +416,10 @@
     for copies in hops0 + hops1:
         for copy in copies:
             copy.wait_send()
-    turn_wait(0, own_b)
-    turn_wait(1, own_u)
-    got_b = lane_blocks([xrecv[0, i] for i in range(4)])
-    got_u = lane_blocks([xrecv[1, i] for i in range(4)])
-    for i in range(4):
-        ctl[pl.ds(i, 128, stride=4), :] = c_b * got_b[i] + c_u * got_u[i]
+    turn_wait(1, own_u[0])
     for p in range(32):
-        control_out[0, :, p * 128 : p * 128 + 128] = ctl[p * 16 : p * 16 + 16, :]
+        rows = slice(p * 16, p * 16 + 16)
+        control_out[0, :, p * 128 : p * 128 + 128] = c_b * ctl[0, rows, :] + c_u * ctl[1, rows, :]
 
 
 def body(background_std, x_kernel, y_kernel, obs_owner, obs_cells, obs_weights, innovation, obs_precision, obs_counts):
@@ -455,7 +452,7 @@
             pltpu.VMEM((512, 256), F32),
             pltpu.VMEM((2, 256, 256), F32), pltpu.VMEM((2, 256, 256), F32), pltpu.VMEM((2, 256, 256), F32),
             field, field, field, field, field,
-            pltpu.VMEM((128, 128), F32), pltpu.VMEM((512, 128), F32),
+            pltpu.VMEM((128, 128), F32), pltpu.VMEM((2, 512, 128), F32),
             pltpu.VMEM((2, 512, 128), F32), pltpu.VMEM((2, 4, 128, 128), F32),
             pltpu.VMEM((1, 1, 128), F32), pltpu.VMEM((NEAR, 1, 128), F32),
             pltpu.VMEM((1, 1, 128), F32), pltpu.VMEM((FAR_Y * LEVS, 1, 128), F32),

time: 68.7 us -> 64.9 us (0.945)
  Pallas kernels: 65.9 us -> 62.1 us
    pallas_call x1, Pallas kernels: 65.9 us -> 62.1 us  [body(): pl.pallas_call(kernel, out_shape=(jax.ShapeDtypeStruct((1, 16, 4096), F32...]
where the time goes in v3:
time: 64.9 us; the launch traced here: 64.8 us
  Pallas kernels  62.1 us (96%)
  local copies, waits for them, and re-layouts  1.41 us (2%)
  between operations  1.29 us (2%)
    pallas_call x1, Pallas kernels, body(): pl.pallas_call(kernel, out_shape=(jax.ShapeDtypeStruct((1, 16, 4096), F32...  62.1 us
    unnamed x2, local copies, waits for them, and re-layouts  1.41 us

profile of v3, /device:TPU:1, one launch (start us, length us, event | category | flops | bytes accessed | tf_op | source)
XLA Modules:
  0.0 64.8 jit_solution(13769309797908584904)
XLA Ops:
  1.3 62.1 %assimilate.1 = (f32[1,16,4096]{2,1,0:T(8,128)S(1)}, f32[1,32,2048]{2,1,0:T(8,128)S(1)}) custom-call(f32[1,32,2048]{2,1,0:T(8,128)} %std_hbm.1, f32[1,31]{1,0:T(1,128)} %xk_hbm.1, f32[1,31]{1,0:T(1,128)} %yk_hbm.1, s32[1,256]{1,0:T(1,128)} %bitcast.9, s32[16,256]{1,0:T(8,128)} %bitcast.7, f32[16,256]{1,0:T(8,128)} %bitcast.8, f32[1,256]{1,0:T(1,128)} %bitcast.10, ...), custom_call_target="tpu_custom_call" | custom-call | tf_op jit(solution)/shard_map/assimilate/pallas_call | solution.py:432
  63.4 0.7 %copy.14 = f32[1,16,4096]{2,1,0:T(8,128)} copy(f32[1,16,4096]{2,1,0:T(8,128)S(1)} %get-tuple-element.4) | data formatting | bytes 524288
  64.1 0.7 %copy.15 = f32[1,32,2048]{2,1,0:T(8,128)} copy(f32[1,32,2048]{2,1,0:T(8,128)S(1)} %get-tuple-element.5) | data formatting | bytes 524288

commit v4 on v3

--- a/solution.py
+++ b/solution.py
@@ -84,6 +84,18 @@
         for zc in zcs[:-1]:
             act(row * NEAR + zc)
 
+    barrier = pltpu.get_barrier_semaphore()
+
+    def hello(q, to_lev=lev):
+        pl.semaphore_signal(barrier, inc=1, device_id=(q, to_lev), device_id_type=MESH)
+
+    each_peer(hello)
+
+    @pl.loop(0, FAR_Y)
+    def _(i):
+        for dx in (2, 1, 3):
+            hello(lax.rem(row + FAR_Y // 2 + i, FAR_Y) * NEAR + near, lax.rem(lev + dx, LEVS))
+
     loads = [
         pltpu.make_async_copy(src, dst, isem.at[i])
         for i, (src, dst) in enumerate(
@@ -95,18 +107,6 @@
     ]
     for load in loads:
         load.start()
-    barrier = pltpu.get_barrier_semaphore()
-
-    def hello(q, to_lev=lev):
-        pl.semaphore_signal(barrier, inc=1, device_id=(q, to_lev), device_id_type=MESH)
-
-    each_peer(hello)
-
-    @pl.loop(0, FAR_Y)
-    def _(i):
-        for dx in (2, 1, 3):
-            hello(lax.rem(row + FAR_Y // 2 + i, FAR_Y) * NEAR + near, lax.rem(lev + dx, LEVS))
-
     for load in loads[:6]:
         load.wait()
 
@@ -267,7 +267,7 @@
             copies.append(both)
         return copies
 
-    def along_x(n, copies, out):
+    def along_x(n, copies, out, halfway=None):
         for c in range(CHUNKS):
             for copy in copies[c]:
                 copy.wait_recv()
@@ -279,23 +279,44 @@
                 r = r1[0:64] + r1[64:128] + dot(ax_ref[0:64, :], lo)
                 out[rows, :] = r[0:32]
                 vbuf[rows, :] = r[32:64]
+            if halfway and 2 * (c + 1) == CHUNKS:
+                halfway()
 
     pp, p4 = lax.rem(me, 4), lax.div(me, 4) * 4
 
-    def turn(f, buf):
-        for g in range(2):
-            for h in range(2):
-                turned[...] = buf[g * 128 : g * 128 + 128, h * 128 : h * 128 + 128].T
-                x = [turned[pl.ds(i, 32, stride=4), :] for i in range(4)]
-                for t, m in enumerate(lane_blocks(x)):
-                    at = ((4 * g + t) * 16 + h * 8) * 4
-                    xsend[f, at : at + 32, :] = m
+    def turn_half(f, buf, g):
+        for h in range(2):
+            turned[...] = buf[g * 128 : g * 128 + 128, h * 128 : h * 128 + 128].T
+            x = [turned[pl.ds(i, 32, stride=4), :] for i in range(4)]
+            for t, m in enumerate(lane_blocks(x)):
+                at = ((4 * g + t) * 16 + h * 8) * 4
+                xsend[f, at : at + 32, :] = m
+
+    def turn_own(f):
         mine = pltpu.make_async_copy(
             xsend.at[f, pl.ds(me * 4, 4)], xrecv.at[f, pp, pl.ds(p4, 4)], lsem.at[1 + f]
         )
         mine.start()
+        return mine
+
+    def turn(f, buf):
+        turn_half(f, buf, 0)
+        turn_half(f, buf, 1)
+        mine = turn_own(f)
         each_peer(lambda q: turn_copy(f, q).start())
         return mine
+
+    def send_half(f, g):
+        half = PENCILS // 2
+
+        @pl.loop(0, 7)
+        def _(o):
+            for j in range(9):
+                turn_copy(f, half * g + lax.rem(me + 1 + 9 * o + j, half)).start()
+
+        @pl.when(lax.div(me, half) != g)
+        def _():
+            turn_copy(f, half * g + lax.rem(me, half)).start()
 
     def turn_copy(f, q):
         return pltpu.make_async_remote_copy(
@@ -323,10 +344,15 @@
         for i, m in enumerate(lane_blocks([xrecv[f, i] for i in range(4)])):
             ctl[f, pl.ds(i, 128, stride=4), :] = m
 
+    def turn_b(g):
+        turn_half(0, bbuf, g)
+        send_half(0, g)
+
     hops0 = halo(0, wd)
-    along_x(0, hops0, bbuf)
+    along_x(0, hops0, bbuf, lambda: turn_b(0))
     bb_f[...] = std[...] * dot(y_operand(vbuf[...]), ty[...])
-    own_b = turn(0, bbuf)
+    turn_b(1)
+    own_b = turn_own(0)
     y0 = observe(bb_f[...])
     hops1 = halo(1, wgt * y0)
     along_x(1, hops1, ubuf)

time: 64.9 us -> 64.5 us (level)
  no operation moved by 1% of the time
where the time goes in v4:
time: 64.5 us; the launch traced here: 64.4 us
  Pallas kernels  61.7 us (96%)
  local copies, waits for them, and re-layouts  1.41 us (2%)
  between operations  1.29 us (2%)
    pallas_call x1, Pallas kernels, body(): pl.pallas_call(kernel, out_shape=(jax.ShapeDtypeStruct((1, 16, 4096), F32...  61.7 us
    unnamed x2, local copies, waits for them, and re-layouts  1.41 us

profile of v4, /device:TPU:1, one launch (start us, length us, event | category | flops | bytes accessed | tf_op | source)
XLA Modules:
  0.0 64.4 jit_solution(13604579079684642562)
XLA Ops:
  1.3 61.7 %assimilate.1 = (f32[1,16,4096]{2,1,0:T(8,128)S(1)}, f32[1,32,2048]{2,1,0:T(8,128)S(1)}) custom-call(f32[1,32,2048]{2,1,0:T(8,128)} %std_hbm.1, f32[1,31]{1,0:T(1,128)} %xk_hbm.1, f32[1,31]{1,0:T(1,128)} %yk_hbm.1, s32[1,256]{1,0:T(1,128)} %bitcast.9, s32[16,256]{1,0:T(8,128)} %bitcast.7, f32[16,256]{1,0:T(8,128)} %bitcast.8, f32[1,256]{1,0:T(1,128)} %bitcast.10, ...), custom_call_target="tpu_custom_call" | custom-call | tf_op jit(solution)/shard_map/assimilate/pallas_call | solution.py:458
  62.9 0.7 %copy.14 = f32[1,16,4096]{2,1,0:T(8,128)} copy(f32[1,16,4096]{2,1,0:T(8,128)S(1)} %get-tuple-element.4) | data formatting | bytes 524288
  63.7 0.7 %copy.15 = f32[1,32,2048]{2,1,0:T(8,128)} copy(f32[1,32,2048]{2,1,0:T(8,128)S(1)} %get-tuple-element.5) | data formatting | bytes 524288
